TPU v7x, 256 devices: a whole 4x4x8 slice. The times are simulated.
256 devices in a mesh: row: 32 (over y, x, core), col: 8 (over z).
Axes of the slice: x: 4, y: 4, z: 8, core: 2. Of those that a mesh axis runs over, the one named last changes fastest.
Arguments:
- inputs: bfloat16 [768, 12288], P(None, 'col'), may hold values from -6 to 6
- out_grad: bfloat16 [768, 12288], P(None, 'col'), may hold values from -6 to 6
- pre_act: bfloat16 [768, 24576], P('col', 'row'), may hold values from -8 to 8
- w_in: bfloat16 [12288, 24576], P('col', 'row'), may hold values from -0.0546875 to 0.0546875
- w_out: bfloat16 [24576, 12288], P('row', 'col'), may hold values from -0.0390625 to 0.0390625
Outputs:
- grad_inputs: bfloat16 [768, 12288], P('row', 'col')
- grad_w_in: bfloat16 [12288, 24576], P('col', 'row')
- grad_w_out: bfloat16 [24576, 12288], P('row', 'col')
All inputs are finite; a program needn't handle non-finite values.
Results may differ from a plain program's by a relative error of at most 0.0049.
Values may be sent and summed in bfloat16 or wider, within the bound.
A program may use at most 64 MiB of HBM per device.

v0:
```python
import math
import jax
import jax.numpy as jnp
from jax import lax
from jax.sharding import PartitionSpec as P

coef_c = math.sqrt(2.0 / math.pi)


def gelu_parts(pre_values):
    hval = pre_values.astype(jnp.float32)
    tval = jnp.tanh(coef_c * (hval + 0.044715 * hval * hval * hval))
    activ = 0.5 * hval * (1.0 + tval)
    deriv = 0.5 * (1.0 + tval) + 0.5 * hval * (1.0 - tval * tval) * coef_c * (
        1.0 + 3.0 * 0.044715 * hval * hval
    )
    return (activ, deriv)


def per_device(inputs, out_grad, pre_act, w_in, w_out):
    total_tokens = inputs.shape[0]
    scale_value = 1.0 / math.sqrt(total_tokens)
    block = out_grad
    act_share = lax.psum_scatter(
        lax.dot_general(block, w_out, (((1,), (1,)), ((), ())), preferred_element_type=jnp.float32),
        "col",
        scatter_dimension=0,
        tiled=True,
    )
    local_act, local_deriv = gelu_parts(pre_act)
    hid_share = (act_share * local_deriv).astype(jnp.bfloat16)
    activ_all, hid_all = (
        lax.all_gather(local_act.astype(jnp.bfloat16), "col", axis=0, tiled=True),
        lax.all_gather(hid_share, "col", axis=0, tiled=True),
    )
    grad_w_out = lax.dot_general(
        activ_all, out_grad, (((0,), (0,)), ((), ())), preferred_element_type=jnp.float32
    )
    grad_w_out = (grad_w_out * scale_value).astype(jnp.bfloat16)
    grad_w_in = lax.dot_general(
        inputs, hid_all, (((0,), (0,)), ((), ())), preferred_element_type=jnp.float32
    )
    grad_w_in = (grad_w_in * scale_value).astype(jnp.bfloat16)
    block = hid_all
    grad_inputs = lax.psum_scatter(
        lax.dot_general(block, w_in, (((1,), (1,)), ((), ())), preferred_element_type=jnp.float32),
        "row",
        scatter_dimension=0,
        tiled=True,
    )
    return (grad_inputs.astype(jnp.bfloat16), grad_w_in, grad_w_out)


def solution(mesh):
    placed = (P(None, "col"), P(None, "col"), P("col", "row"), P("col", "row"), P("row", "col"))
    return jax.shard_map(
        per_device,
        mesh=mesh,
        in_specs=placed,
        out_specs=(P("row", "col"), P("col", "row"), P("row", "col")),
        check_vma=False,
    )
```

profile of v0, /device:TPU:2, one launch (start us, length us, event | category | flops | bytes accessed | tf_op | source)
XLA Modules:
  0.0 241.4 jit_solution(5547403851123938522)
XLA Ops:
  7.2 0.0 copy-start
  7.2 0.0 reduce-scatter.3.cloned.1.call-start
  7.2 1.6 copy-done
  8.8 5.1 %fusion.12 = f32[768,768]{1,0:T(8,128)} fusion(bf16[768,1536]{1,0:T(8,128)(2,1)S(1)} %copy-done, bf16[768,1536]{1,0:T(8,128)(2,1)} %param.9), kind=kOutput, calls=%fused_computation.21 | convolution fusion | flops 1811939328 | bytes 7077888 | tf_op jit(solution)/shard_map/dot_general | solution.py:25
  13.9 0.0 copy-start.1
  13.9 0.0 reduce-scatter.3.cloned.1.call-update
  13.9 0.0 all-gather.3.cloned.1.call-start
  14.0 46.3 %reduce-scatter.3.cloned.1.call-done = f32[96,768]{1,0:T(8,128)} async-done(((f32[768,768]{1,0:T(8,128)}), f32[96,768]{1,0:T(8,128)}) %reduce-scatter.3.cloned.1.call-update) | async-done | bytes 294928 | tf_op jit(solution)/shard_map/reduce_scatter | solution.py:24
  60.3 0.0 copy-done.1
  60.3 1.9 fusion.8
  62.1 0.0 all-gather.3.cloned.1.call-update
  62.2 0.0 all-gather.5.cloned.1.call-start
  62.2 0.7 all-gather.5.cloned.1.call-update
  62.9 0.0 reduce-scatter.5.cloned.1.call-start
  63.0 37.7 %all-gather.3.cloned.1.call-done = bf16[768,768]{1,0:T(8,128)(2,1)} async-done(((bf16[96,768]{1,0:T(8,128)(2,1)}), bf16[768,768]{1,0:T(8,128)(2,1)}) %all-gather.3.cloned.1.call-update) | async-done | bytes 1179664 | tf_op jit(solution)/shard_map/all_gather | solution.py:34
  100.7 6.2 %fusion.13 = f32[768,1536]{1,0:T(8,128)} fusion(bf16[768,768]{1,0:T(8,128)(2,1)} %all-gather.3.cloned.1.call-done, bf16[1536,768]{1,0:T(8,128)(2,1)} %param.8), kind=kOutput, calls=%fused_computation.22 | convolution fusion | flops 1811939328 | bytes 8257536 | tf_op jit(solution)/shard_map/dot_general | solution.py:46
  106.9 0.0 reduce-scatter.5.cloned.1.call-update
  106.9 1.2 copy-done.2
  108.1 5.1 %fusion = bf16[1536,768]{0,1:T(8,128)(2,1)} fusion(bf16[768,768]{1,0:T(8,128)(2,1)S(1)} %copy-done.2, bf16[768,1536]{1,0:T(8,128)(2,1)} %param.5), kind=kOutput, calls=%fused_computation.2 | convolution fusion | flops 1814298624 | bytes 5898240 | tf_op jit(solution)/shard_map/dot_general | solution.py:40
  113.2 4.3 %copy.8 = bf16[1536,768]{1,0:T(8,128)(2,1)} copy(bf16[1536,768]{0,1:T(8,128)(2,1)} %fusion) | data formatting | bytes 4718592
  117.5 22.2 %all-gather.5.cloned.1.call-done = bf16[768,768]{1,0:T(8,128)(2,1)} async-done(((bf16[96,768]{1,0:T(8,128)(2,1)}), bf16[768,768]{1,0:T(8,128)(2,1)}) %all-gather.5.cloned.1.call-update) | async-done | bytes 1179664 | tf_op jit(solution)/shard_map/all_gather | solution.py:33
  139.7 4.7 %multiply_convert_fusion = bf16[768,1536]{1,0:T(8,128)(2,1)} fusion(bf16[768,768]{1,0:T(8,128)(2,1)} %all-gather.5.cloned.1.call-done, bf16[768,1536]{1,0:T(8,128)(2,1)S(1)} %copy-done), kind=kOutput, calls=%fused_computation | convolution fusion | flops 1814298624 | bytes 5898240 | tf_op jit(solution)/shard_map/dot_general | solution.py:36
  144.4 88.9 %reduce-scatter.5.cloned.1.call-done = f32[24,1536]{1,0:T(8,128)} async-done(((f32[768,1536]{1,0:T(8,128)}), f32[24,1536]{1,0:T(8,128)}) %reduce-scatter.5.cloned.1.call-update) | async-done | bytes 147472 | tf_op jit(solution)/shard_map/reduce_scatter | solution.py:45
  233.3 1.6 convert_element_type.23
  (1 shorter events, 0.0 us)
Async XLA Ops:
  7.2 1.7 copy-start
  7.2 53.1 %reduce-scatter.3.cloned.1.call-start = ((), (), s32[]{:S(2)}) async-start(), calls=%async_computation.2 | async-start | bytes 2654208 | tf_op jit(solution)/shard_map/reduce_scatter | solution.py:24
  13.9 46.3 %copy-start.1 = (bf16[96,768]{1,0:T(8,128)(2,1)S(1)}, bf16[96,768]{1,0:T(8,128)(2,1)}, u32[]{:S(2)}) copy-start(bf16[96,768]{1,0:T(8,128)(2,1)} %param.7) | copy-start | bytes 442372
  13.9 86.7 %all-gather.3.cloned.1.call-start = ((), (), s32[]{:S(2)}) async-start(), calls=%async_computation.3 | async-start | bytes 1327104 | tf_op jit(solution)/shard_map/all_gather | solution.py:34
  62.2 77.6 %all-gather.5.cloned.1.call-start = ((), (), s32[]{:S(2)}) async-start(), calls=%async_computation.5 | async-start | bytes 1327104 | tf_op jit(solution)/shard_map/all_gather | solution.py:33
  62.9 170.4 %reduce-scatter.5.cloned.1.call-start = ((), (), s32[]{:S(2)}) async-start(), calls=%async_computation.4 | async-start | bytes 4866048 | tf_op jit(solution)/shard_map/reduce_scatter | solution.py:45
  106.9 1.3 copy-start.2
Sparse Core Ops, SparseCore 0:
  14.1 46.1 reduce-scatter.2
  62.6 37.9 all-gather.2
  102.5 37.2 all-gather.4
  143.6 89.6 reduce-scatter.4
where the time goes:
time: 242 us; the launch traced here: 241 us
  waiting for transfers between devices  196 us (81%)
  matrix products  21.1 us (9%)
  between operations  13.8 us (6%)
  local copies, waits for them, and re-layouts  7.13 us (3%)
  other arithmetic  3.43 us (1%)
    reduce_scatter x1, waiting for transfers between devices, per_device(): lax.psum_scatter(lax.dot_general(block, w_in, (((1,), (1,)), ((), ())), p...  88.9 us
    reduce_scatter x1, waiting for transfers between devices, per_device(): lax.psum_scatter(lax.dot_general(block, w_out, (((1,), (1,)), ((), ())),...  46.3 us
    all_gather x1, waiting for transfers between devices, per_device(): lax.all_gather(hid_share, 'col', axis=0, tiled=True)  37.7 us
    all_gather x1, waiting for transfers between devices, per_device(): lax.all_gather(local_act.astype(jnp.bfloat16), 'col', axis=0, tiled=True)  22.2 us
    unnamed x7, local copies, waits for them, and re-layouts  7.13 us
    dot_general x1, matrix products, per_device(): lax.dot_general(block, w_in, (((1,), (1,)), ((), ())), preferred_element_...  6.2 us
    dot_general x1, matrix products, per_device(): lax.dot_general(inputs, hid_all, (((0,), (0,)), ((), ())), preferred_elem...  5.1 us
    dot_general x1, matrix products, per_device(): lax.dot_general(block, w_out, (((1,), (1,)), ((), ())), preferred_element...  5.09 us
  transfers between devices with their start and end apart: 4, of which 4 were waited for; matrix products, arithmetic and copies ran while one was open for 8% of the time, Pallas kernels for 0%

commit v1 on v0

--- a/solution.py
+++ b/solution.py
@@ -18,6 +18,34 @@
 
 
 def per_device(inputs, out_grad, pre_act, w_in, w_out):
+
+    def meet_keys(x_local):
+        a_name = "col"
+        now = lax.psum(1, a_name)
+        current_arr, local_out, front = (now, lax.axis_index(a_name), x_local.shape[0])
+        carry = jnp.zeros(
+            [j * current_arr if jj == 0 else j for jj, j in enumerate(x_local.shape)], x_local.dtype
+        )
+        response = lax.dynamic_update_slice_in_dim(carry, x_local, local_out * front, axis=0)
+        r2 = res = x_local
+        nth = 1
+        while nth < current_arr // 2 + 1:
+            r2 = lax.ppermute(
+                r2, a_name, [(jj, (jj + 1) % current_arr) for jj in range(current_arr)]
+            )
+            response = lax.dynamic_update_slice_in_dim(
+                response, r2, (local_out - nth) % current_arr * front, axis=0
+            )
+            if 2 * nth < current_arr:
+                res = lax.ppermute(
+                    res, a_name, [(jj, (jj - 1) % current_arr) for jj in range(current_arr)]
+                )
+                response = lax.dynamic_update_slice_in_dim(
+                    response, res, (local_out + nth) % current_arr * front, axis=0
+                )
+            nth = nth + 1
+        return response
+
     total_tokens = inputs.shape[0]
     scale_value = 1.0 / math.sqrt(total_tokens)
     block = out_grad
@@ -31,7 +59,7 @@
     hid_share = (act_share * local_deriv).astype(jnp.bfloat16)
     activ_all, hid_all = (
         lax.all_gather(local_act.astype(jnp.bfloat16), "col", axis=0, tiled=True),
-        lax.all_gather(hid_share, "col", axis=0, tiled=True),
+        meet_keys(hid_share),
     )
     grad_w_out = lax.dot_general(
         activ_all, out_grad, (((0,), (0,)), ((), ())), preferred_element_type=jnp.float32

time: 242 us -> 204 us (0.84)
  waiting for transfers between devices: 196 us -> 147 us
  starting transfers between devices: 0.16 us -> 10.1 us
  local copies, waits for them, and re-layouts: 7.13 us -> 9.61 us
    all_gather x1 -> x0, waiting for transfers between devices: 37.7 us -> none  [per_device(): lax.all_gather(hid_share, 'col', axis=0, tiled=True)]
    all_gather x1, waiting for transfers between devices: 22.2 us -> 0.26 us  [per_device(): lax.all_gather(local_act.astype(jnp.bfloat16), 'col', axis=0, tiled=True)]
    ppermute x0 -> x7, waiting for transfers between devices: none -> 20 us  [the longest x4 20 us: meet_keys(): lax.ppermute(r2, a_name, [(jj, (jj + 1) % current_arr) for jj in range(cu...]
    ppermute x0 -> x7, starting transfers between devices: none -> 9.98 us  [the longest x3 9.15 us: meet_keys(): lax.ppermute(res, a_name, [(jj, (jj - 1) % current_arr) for jj in range(c...]
    reduce_scatter x1, waiting for transfers between devices: 88.9 us -> 81.8 us  [per_device(): lax.psum_scatter(lax.dot_general(block, w_in, (((1,), (1,)), ((), ())), p...]
    unnamed x7 -> x9, local copies, waits for them, and re-layouts: 7.13 us -> 7.6 us
  transfers between devices with their start and end apart: 4 -> 10, of which waited for: 4 -> 7; matrix products, arithmetic and copies ran while one was open for 8% -> 11% of each run, Pallas kernels for 0% -> 0%
where the time goes in v1:
time: 204 us
  waiting for transfers between devices  147 us (72%)
  matrix products  19.2 us (9%)
  between operations  13.8 us (7%)
  starting transfers between devices  10.1 us (5%)
  local copies, waits for them, and re-layouts  9.61 us (5%)
  other arithmetic  4.09 us (2%)
    reduce_scatter x1, waiting for transfers between devices, per_device(): lax.psum_scatter(lax.dot_general(block, w_in, (((1,), (1,)), ((), ())), p...  81.8 us
    reduce_scatter x1, waiting for transfers between devices, per_device(): lax.psum_scatter(lax.dot_general(block, w_out, (((1,), (1,)), ((), ())),...  44.6 us
    ppermute x4, waiting for transfers between devices, meet_keys(): lax.ppermute(r2, a_name, [(jj, (jj + 1) % current_arr) for jj in range(cu...  20 us
    ppermute x3, starting transfers between devices, meet_keys(): lax.ppermute(res, a_name, [(jj, (jj - 1) % current_arr) for jj in range(c...  9.15 us
    unnamed x9, local copies, waits for them, and re-layouts  7.6 us
    dot_general x1, matrix products, per_device(): lax.dot_general(block, w_in, (((1,), (1,)), ((), ())), preferred_element_...  5.82 us
    dot_general x1, matrix products, per_device(): lax.dot_general(block, w_out, (((1,), (1,)), ((), ())), preferred_element...  5.09 us
    dot_general x1, matrix products, per_device(): lax.dot_general(activ_all, out_grad, (((0,), (0,)), ((), ())), preferred_...  4.85 us
  transfers between devices with their start and end apart: 10, of which 7 were waited for; matrix products, arithmetic and copies ran while one was open for 11% of the time, Pallas kernels for 0%

profile of v1, /device:TPU:2, one launch (start us, length us, event | category | flops | bytes accessed | tf_op | source)
XLA Modules:
  0.0 203.6 jit_solution(272559569247811881)
XLA Ops:
  7.2 1.6 copy-done
  8.8 5.1 %fusion.13 = f32[768,768]{1,0:T(8,128)} fusion(bf16[768,1536]{1,0:T(8,128)(2,1)S(1)} %copy-done, bf16[768,1536]{1,0:T(8,128)(2,1)} %param.9), kind=kOutput, calls=%fused_computation.29 | convolution fusion | flops 1811939328 | bytes 7077888 | tf_op jit(solution)/shard_map/dot_general | solution.py:53
  14.0 0.8 copy-done.1
  14.8 0.8 fusion.8
  15.7 44.6 %reduce-scatter.3.cloned.1.call-done = f32[96,768]{1,0:T(8,128)} async-done(((f32[768,768]{1,0:T(8,128)}), f32[96,768]{1,0:T(8,128)}) %reduce-scatter.3.cloned.1.call-update) | async-done | bytes 294928 | tf_op jit(solution)/shard_map/reduce_scatter | solution.py:52
  60.4 0.9 copy-done.2
  61.3 1.8 constant_dynamic-update-slice_fusion.7
  63.0 0.8 collective-permute-start
  63.9 2.4 %collective-permute-start.1 = (bf16[96,768]{1,0:T(8,128)(2,1)}, bf16[96,768]{1,0:T(8,128)(2,1)}, u32[]{:S(2)}, u32[]{:S(2)}) collective-permute-start(bf16[96,768]{1,0:T(8,128)(2,1)} %get-tuple-element.7), channel_id=1, source_target_pairs={{0,7},{1,0},{2,1},{3,2},{4,3},{5,4},{6,5},{7,6},{8,15},{9,8},{10,9... | collective-permute-start | bytes 442376 | tf_op jit(solution)/shard_map/ppermute | solution.py:40
  66.3 4.6 %collective-permute-done = bf16[96,768]{1,0:T(8,128)(2,1)} collective-permute-done((bf16[96,768]{1,0:T(8,128)(2,1)}, bf16[96,768]{1,0:T(8,128)(2,1)}, u32[]{:S(2)}, u32[]{:S(2)}) %collective-permute-start) | collective-permute-done | bytes 147488 | tf_op jit(solution)/shard_map/ppermute | solution.py:33
  70.9 3.5 %collective-permute-start.3 = (bf16[96,768]{1,0:T(8,128)(2,1)}, bf16[96,768]{1,0:T(8,128)(2,1)S(1)}, u32[]{:S(2)}, u32[]{:S(2)}) collective-permute-start(bf16[96,768]{1,0:T(8,128)(2,1)} %collective-permute-done.1), channel_id=1, source_target_pairs={{0,7},{1,0},{2,1},{3,2},{4,3},{5,4},{6,5},{7,6},{8,15},{9,8},{10,9... | collective-permute-start | bytes 442376 | tf_op jit(solution)/shard_map/ppermute | solution.py:40
  74.4 0.9 constant_dynamic-update-slice_fusion.6
  75.3 0.9 constant_dynamic-update-slice_fusion.5
  76.3 3.3 %collective-permute-done.2 = bf16[96,768]{1,0:T(8,128)(2,1)S(1)} collective-permute-done((bf16[96,768]{1,0:T(8,128)(2,1)}, bf16[96,768]{1,0:T(8,128)(2,1)S(1)}, u32[]{:S(2)}, u32[]{:S(2)}) %collective-permute-start.2) | collective-permute-done | bytes 147488 | tf_op jit(solution)/shard_map/ppermute | solution.py:33
  79.6 3.2 %collective-permute-start.5 = (bf16[96,768]{1,0:T(8,128)(2,1)S(1)}, bf16[96,768]{1,0:T(8,128)(2,1)S(1)}, u32[]{:S(2)}, u32[]{:S(2)}) collective-permute-start(bf16[96,768]{1,0:T(8,128)(2,1)S(1)} %collective-permute-done.3), channel_id=1, source_target_pairs={{0,7},{1,0},{2,1},{3,2},{4,3},{5,4},{6,5},{7,6},{8,15},{9,8},{10,9... | collective-permute-start | bytes 442376 | tf_op jit(solution)/shard_map/ppermute | solution.py:40
  82.9 4.5 %collective-permute-done.4 = bf16[96,768]{1,0:T(8,128)(2,1)S(1)} collective-permute-done((bf16[96,768]{1,0:T(8,128)(2,1)S(1)}, bf16[96,768]{1,0:T(8,128)(2,1)S(1)}, u32[]{:S(2)}, u32[]{:S(2)}) %collective-permute-start.4) | collective-permute-done | bytes 147488 | tf_op jit(solution)/shard_map/ppermute | solution.py:33
  87.5 7.5 %collective-permute-done.6 = bf16[96,768]{1,0:T(8,128)(2,1)S(1)} collective-permute-done((bf16[96,768]{1,0:T(8,128)(2,1)S(1)}, bf16[96,768]{1,0:T(8,128)(2,1)S(1)}, u32[]{:S(2)}, u32[]{:S(2)}) %collective-permute-start.6) | collective-permute-done | bytes 147488 | tf_op jit(solution)/shard_map/ppermute | solution.py:33
  95.0 5.8 %fusion.14 = f32[768,1536]{1,0:T(8,128)} fusion(bf16[768,768]{1,0:T(8,128)(2,1)S(1)} %constant_dynamic-update-slice_fusion, bf16[1536,768]{1,0:T(8,128)(2,1)} %param.8), kind=kOutput, calls=%fused_computation.30 | convolution fusion | flops 1811939328 | bytes 8257536 | tf_op jit(solution)/shard_map/dot_general | solution.py:74
  100.8 0.3 all-gather.2.cloned.1.call-done
  101.1 4.9 %multiply_convert_fusion = bf16[768,1536]{1,0:T(8,128)(2,1)} fusion(bf16[768,768]{1,0:T(8,128)(2,1)} %all-gather.2.cloned.1.call-done, bf16[768,1536]{1,0:T(8,128)(2,1)S(1)} %copy-done), kind=kOutput, calls=%fused_computation | convolution fusion | flops 1814298624 | bytes 5898240 | tf_op jit(solution)/shard_map/dot_general | solution.py:64
  105.9 3.5 %fusion = bf16[1536,768]{0,1:T(8,128)(2,1)} fusion(bf16[768,768]{1,0:T(8,128)(2,1)S(1)} %constant_dynamic-update-slice_fusion, bf16[768,1536]{1,0:T(8,128)(2,1)S(1)} %copy-done.3), kind=kOutput, calls=%fused_computation.2 | convolution fusion | flops 1814298624 | bytes 5898240 | tf_op jit(solution)/shard_map/dot_general | solution.py:68
  109.4 4.3 %copy.8 = bf16[1536,768]{1,0:T(8,128)(2,1)} copy(bf16[1536,768]{0,1:T(8,128)(2,1)} %fusion) | data formatting | bytes 4718592
  113.7 81.8 %reduce-scatter.5.cloned.1.call-done = f32[24,1536]{1,0:T(8,128)} async-done(((f32[768,1536]{1,0:T(8,128)}), f32[24,1536]{1,0:T(8,128)}) %reduce-scatter.5.cloned.1.call-update) | async-done | bytes 147472 | tf_op jit(solution)/shard_map/reduce_scatter | solution.py:73
  195.5 1.6 convert_element_type.23
  (23 shorter events, 0.4 us)
Async XLA Ops:
  7.2 1.7 copy-start
  7.2 53.1 %reduce-scatter.3.cloned.1.call-start = ((), (), s32[]{:S(2)}) async-start(), calls=%async_computation.2 | async-start | bytes 2654208 | tf_op jit(solution)/shard_map/reduce_scatter | solution.py:52
  13.9 0.9 copy-start.1
  14.0 87.1 %all-gather.2.cloned.1.call-start = ((), (), s32[]{:S(2)}) async-start(), calls=%async_computation.4 | async-start | bytes 1327104 | tf_op jit(solution)/shard_map/all_gather | solution.py:61
  15.6 179.9 %reduce-scatter.5.cloned.1.call-start = ((), (), s32[]{:S(2)}) async-start(), calls=%async_computation.3 | async-start | bytes 4866048 | tf_op jit(solution)/shard_map/reduce_scatter | solution.py:73
  60.3 1.0 copy-start.2
  63.0 7.9 %collective-permute-start = (bf16[96,768]{1,0:T(8,128)(2,1)}, bf16[96,768]{1,0:T(8,128)(2,1)}, u32[]{:S(2)}, u32[]{:S(2)}) collective-permute-start(bf16[96,768]{1,0:T(8,128)(2,1)} %get-tuple-element.7), channel_id=1, source_target_pairs={{0,1},{1,2},{2,3},{3,4},{4,5},{5,6},{6,7},{7,0},{8,9},{9,10},{10,1... | collective-permute-start | bytes 442376 | tf_op jit(solution)/shard_map/ppermute | solution.py:33
  63.9 7.1 %collective-permute-start.1 = (bf16[96,768]{1,0:T(8,128)(2,1)}, bf16[96,768]{1,0:T(8,128)(2,1)}, u32[]{:S(2)}, u32[]{:S(2)}) collective-permute-start(bf16[96,768]{1,0:T(8,128)(2,1)} %get-tuple-element.7), channel_id=1, source_target_pairs={{0,7},{1,0},{2,1},{3,2},{4,3},{5,4},{6,5},{7,6},{8,15},{9,8},{10,9... | collective-permute-start | bytes 442376 | tf_op jit(solution)/shard_map/ppermute | solution.py:40
  70.9 8.7 %collective-permute-start.2 = (bf16[96,768]{1,0:T(8,128)(2,1)}, bf16[96,768]{1,0:T(8,128)(2,1)S(1)}, u32[]{:S(2)}, u32[]{:S(2)}) collective-permute-start(bf16[96,768]{1,0:T(8,128)(2,1)} %collective-permute-done), channel_id=1, source_target_pairs={{0,1},{1,2},{2,3},{3,4},{4,5},{5,6},{6,7},{7,0},{8,9},{9,10},{10,1... | collective-permute-start | bytes 442376 | tf_op jit(solution)/shard_map/ppermute | solution.py:33
  70.9 8.7 %collective-permute-start.3 = (bf16[96,768]{1,0:T(8,128)(2,1)}, bf16[96,768]{1,0:T(8,128)(2,1)S(1)}, u32[]{:S(2)}, u32[]{:S(2)}) collective-permute-start(bf16[96,768]{1,0:T(8,128)(2,1)} %collective-permute-done.1), channel_id=1, source_target_pairs={{0,7},{1,0},{2,1},{3,2},{4,3},{5,4},{6,5},{7,6},{8,15},{9,8},{10,9... | collective-permute-start | bytes 442376 | tf_op jit(solution)/shard_map/ppermute | solution.py:40
  79.6 7.8 %collective-permute-start.4 = (bf16[96,768]{1,0:T(8,128)(2,1)S(1)}, bf16[96,768]{1,0:T(8,128)(2,1)S(1)}, u32[]{:S(2)}, u32[]{:S(2)}) collective-permute-start(bf16[96,768]{1,0:T(8,128)(2,1)S(1)} %collective-permute-done.2), channel_id=1, source_target_pairs={{0,1},{1,2},{2,3},{3,4},{4,5},{5,6},{6,7},{7,0},{8,9},{9,10},{10,1... | collective-permute-start | bytes 442376 | tf_op jit(solution)/shard_map/ppermute | solution.py:33
  79.6 7.8 %collective-permute-start.5 = (bf16[96,768]{1,0:T(8,128)(2,1)S(1)}, bf16[96,768]{1,0:T(8,128)(2,1)S(1)}, u32[]{:S(2)}, u32[]{:S(2)}) collective-permute-start(bf16[96,768]{1,0:T(8,128)(2,1)S(1)} %collective-permute-done.3), channel_id=1, source_target_pairs={{0,7},{1,0},{2,1},{3,2},{4,3},{5,4},{6,5},{7,6},{8,15},{9,8},{10,9... | collective-permute-start | bytes 442376 | tf_op jit(solution)/shard_map/ppermute | solution.py:40
  87.4 7.6 %collective-permute-start.6 = (bf16[96,768]{1,0:T(8,128)(2,1)S(1)}, bf16[96,768]{1,0:T(8,128)(2,1)S(1)}, u32[]{:S(2)}, u32[]{:S(2)}) collective-permute-start(bf16[96,768]{1,0:T(8,128)(2,1)S(1)} %collective-permute-done.4), channel_id=1, source_target_pairs={{0,1},{1,2},{2,3},{3,4},{4,5},{5,6},{6,7},{7,0},{8,9},{9,10},{10,1... | collective-permute-start | bytes 442376 | tf_op jit(solution)/shard_map/ppermute | solution.py:33
  101.1 4.9 %copy-start.3 = (bf16[768,1536]{1,0:T(8,128)(2,1)S(1)}, bf16[768,1536]{1,0:T(8,128)(2,1)}, u32[]{:S(2)}) copy-start(bf16[768,1536]{1,0:T(8,128)(2,1)} %param.5) | copy-start | bytes 7077892
Sparse Core Ops, SparseCore 0:
  14.1 46.1 reduce-scatter.2
  62.7 38.3 all-gather.1
  105.1 90.3 reduce-scatter.4
